TPU v7x, 32 devices: a whole 2x2x4 slice. The times are simulated.
32 devices in a mesh: tok: 16 (over z, x, core), lyr: 2 (over y).
Axes of the slice: x: 2, y: 2, z: 4, core: 2. Of those that a mesh axis runs over, the one named last changes fastest.
Arguments:
- feature_codes: bfloat16 [4, 2048, 2, 256], P('lyr', 'tok'), may hold values from 0 to 21, as said below
- block_ids: int32 [4, 2048, 2], P('lyr', 'tok'), may hold values from 0 to 31, all different within a row; in each aligned block of 128 rows (0 to 127, 128 to 255, ..., all dimensions but the last counted through in order) at most 16 rows name the same one
- target_layer: int32 [2048], P('tok'), may hold values from 0 to 3
- request_ids: int32 [2048], P('tok'), may hold values from 0 to 15
- target_resid: bfloat16 [2048, 2304], P('tok'), may hold values from -6 to 6
- decoder: bfloat16 [4, 8192, 2304], P('lyr', 'tok'), may hold values from -0.25 to 0.25
Outputs:
- scores: bfloat16 [4, 2048, 2, 256], P('lyr', 'tok')
- request_totals: float32 [16, 4, 8192], P(None, 'lyr', 'tok')
Inputs may be any that keep to these rules, and one draw needn't show every extreme that they name: `block_ids`: the 2 panel indices of one token at one source layer are distinct; among the 128 tokens of one index of tok at one source layer no panel is named by more than 16 of them, a bound that some block reaches. `feature_codes`: nonnegative, with many entries zero.
All inputs are finite; a program needn't handle non-finite values.
Results may differ from a plain program's by a relative error of at most 0.0053.
Values may be sent and summed in bfloat16 or wider, within the bound.
A program may use at most 64 MiB of HBM per device.

v0:
```python
import jax
import jax.numpy as jnp
from jax import lax
from jax.sharding import PartitionSpec as P

PANELS = 32
REQUESTS = 16
CAP = 16


def slot_of(flat_ids):
    one_hot = (flat_ids[:, None] == jnp.arange(PANELS, dtype=jnp.int32)[None, :]).astype(jnp.int32)
    before = jnp.cumsum(one_hot, axis=0) - one_hot
    return flat_ids * CAP + jnp.sum(before * one_hot, axis=1)


def source_of(slot_ids):
    row_count = slot_ids.shape[0]
    empty = jnp.full((PANELS * CAP,), row_count, jnp.int32)
    return empty.at[slot_ids].set(jnp.arange(row_count, dtype=jnp.int32))


def take_rows(table, index):
    return jnp.take(table, index, axis=0)


def pad_zero(table):
    return jnp.concatenate([table, jnp.zeros((1,) + table.shape[1:], table.dtype)], axis=0)


def normalize_error(resid_rows, rebuilt):
    error = resid_rows.astype(jnp.float32) - rebuilt
    spread = jnp.mean(error * error, axis=-1, keepdims=True)
    return (error * lax.rsqrt(spread + 1e-06)).astype(jnp.bfloat16)


def per_device(feature_codes, block_ids, target_layer, request_ids, target_resid, decoder):
    layers_here, count, kact, panel = feature_codes.shape
    width = target_resid.shape[1]
    tok_count = lax.axis_size("tok")
    per_dev = PANELS // tok_count
    rows_here = count * kact
    first_layer = lax.axis_index("lyr") * layers_here
    layer_ids = first_layer + jnp.arange(layers_here, dtype=jnp.int32)
    alive_mask = (layer_ids[:, None] <= target_layer[None, :]).astype(feature_codes.dtype)
    masked = feature_codes * alive_mask[:, :, None, None]
    flat_ids = block_ids.reshape(layers_here, rows_here)
    slot_ids = jax.vmap(slot_of)(flat_ids)
    source_rows = jax.vmap(source_of)(slot_ids)
    token_of = source_rows // kact
    code_rows = jax.vmap(pad_zero)(masked.reshape(layers_here, rows_here, panel))
    send_codes = jax.vmap(take_rows)(code_rows, source_rows).reshape(
        layers_here, tok_count, per_dev, CAP, panel
    )
    panel_weights = decoder.reshape(layers_here, per_dev, panel, width)
    slot_requests = jnp.take(pad_zero(request_ids), token_of, axis=0).reshape(
        layers_here, tok_count, per_dev, CAP
    )
    received, request_slots = (
        lax.all_to_all(send_codes, "tok", split_axis=1, concat_axis=1, tiled=True),
        lax.all_to_all(slot_requests, "tok", split_axis=1, concat_axis=1, tiled=True),
    )
    built = jnp.einsum(
        "lspcj,lpjd->lspcd", received, panel_weights, preferred_element_type=jnp.float32
    ).astype(jnp.bfloat16)
    returned = lax.all_to_all(built, "tok", split_axis=1, concat_axis=1, tiled=True).reshape(
        layers_here, PANELS * CAP, width
    )
    per_row = jax.vmap(take_rows)(returned, slot_ids)
    partial_value = jnp.sum(
        per_row.astype(jnp.float32).reshape(layers_here, count, kact, width), axis=(0, 2)
    )
    rebuilt = lax.psum(partial_value, "lyr")
    gradient = normalize_error(target_resid, rebuilt)
    send_grad = jnp.take(pad_zero(gradient), token_of, axis=0).reshape(
        layers_here, tok_count, per_dev, CAP, width
    )
    received_grad = lax.all_to_all(send_grad, "tok", split_axis=1, concat_axis=1, tiled=True)
    projected_slots = jnp.einsum(
        "lspcd,lpjd->lspcj", received_grad, panel_weights, preferred_element_type=jnp.float32
    ).astype(jnp.bfloat16)
    coming_back = lax.all_to_all(
        projected_slots, "tok", split_axis=1, concat_axis=1, tiled=True
    ).reshape(layers_here, PANELS * CAP, panel)
    picked = jax.vmap(take_rows)(coming_back, slot_ids).reshape(layers_here, count, kact, panel)
    attribution_rows = masked.astype(jnp.float32) * picked.astype(jnp.float32)
    scores = attribution_rows.astype(jnp.bfloat16)
    attribution = received.astype(jnp.float32) * projected_slots.astype(jnp.float32)
    members = (request_slots[..., None] == jnp.arange(REQUESTS, dtype=jnp.int32)).astype(
        jnp.float32
    )
    owned = jnp.einsum("lspcr,lspcj->rlpj", members, attribution, precision=lax.Precision.HIGHEST)
    request_totals = owned.reshape(REQUESTS, layers_here, per_dev * panel)
    return (scores, request_totals)


def solution(mesh):
    placed = (
        P("lyr", "tok", None, None),
        P("lyr", "tok", None),
        P("tok"),
        P("tok"),
        P("tok", None),
        P("lyr", "tok", None),
    )
    return jax.shard_map(
        per_device,
        mesh=mesh,
        in_specs=placed,
        out_specs=(P("lyr", "tok", None, None), P(None, "lyr", "tok")),
        check_vma=False,
    )
```

profile of v0, /device:TPU:0, one launch (start us, length us, event | category | flops | bytes accessed | tf_op | source)
XLA Modules:
  0.0 417.3 jit_solution(11479595752540939134)
XLA Ops:
  7.2 0.0 copy-start.5
  7.2 0.0 copy-start.1
  7.2 0.9 copy.84
  8.0 0.1 eq.39
  8.2 0.1 reshape.141
  8.3 0.7 broadcast_multiply_fusion.1
  9.0 1.2 reduce-window.6
  10.2 0.2 slice_reduce_fusion
  10.5 0.1 copy.89
  10.6 0.1 mul.60
  10.8 0.1 fusion.17
  10.9 24.5 %scatter_fusion = s32[2,512]{1,0:T(2,128)S(1)} fusion(s32[2,512]{1,0:T(2,128)S(1)} %broadcast_in_dim.71, s32[512]{0:T(512)S(1)} %bitcast.74, s32[512]{0:T(512)S(1)} %bitcast.84), kind=kCustom, calls=%fused_computation.5 | custom fusion | bytes 10240 | tf_op jit(solution)/shard_map/vmap()/scatter | solution.py:20
  35.5 0.1 broadcast_in_dim.76
  35.6 0.0 copy-done.5
  35.6 0.1 compare_convert_fusion
  35.7 0.0 copy-done.1
  35.7 0.3 broadcast_multiply_fusion
  36.0 0.4 copy.90
  36.5 0.2 concatenate.9
  36.7 5.5 %gather_fusion.2 = bf16[1024,256]{1,0:T(8,128)(2,1)S(1)} fusion(bf16[2,257,256]{2,0,1:T(2,128)(2,1)S(1)} %concatenate.9, s32[1024]{0:T(1024)S(1)} %bitcast.73), kind=kCustom, calls=%fused_computation.2 | custom fusion | bytes 1056768 | tf_op jit(solution)/shard_map/vmap(jit(_take))/gather | solution.py:24
  42.2 0.2 broadcast_select_fusion.1
  42.4 21.5 %all_to_all.25 = bf16[2,16,2,16,256]{4,3,2,0,1:T(8,128)(2,1)S(1)} all-to-all(bf16[2,16,2,16,256]{4,3,2,0,1:T(8,128)(2,1)S(1)} %copy.91), channel_id=1, replica_groups=mesh['tok'=16,'lyr'=2] {'tok'}, dimensions={1} | all-to-all | bytes 1048576 | tf_op jit(solution)/shard_map/all_to_all | solution.py:60
  63.9 3.7 fusion
  67.6 2.7 copy.93
  70.3 4.6 %all-to-all-start.1 = ((bf16[2,16,2,16,2304]{4,3,2,0,1:T(8,128)(2,1)}), bf16[2,16,2,16,2304]{4,3,2,0,1:T(8,128)(2,1)}, u32[]{:S(2)}, u32[]{:S(2)}) async-start(bf16[2,16,2,16,2304]{4,3,2,0,1:T(8,128)(2,1)} %copy.93), calls=%async_computation.1 | async-start | bytes 9437184 | tf_op jit(solution)/shard_map/all_to_all | solution.py:66
  74.9 0.2 all-reduce.4.cloned.1.call-start
  75.2 86.4 %all-to-all-done.1 = bf16[2,16,2,16,2304]{4,3,2,0,1:T(8,128)(2,1)} async-done(((bf16[2,16,2,16,2304]{4,3,2,0,1:T(8,128)(2,1)}), bf16[2,16,2,16,2304]{4,3,2,0,1:T(8,128)(2,1)}, u32[]{:S(2)}, u32[]{:S(2)}) %all-to-all-start.1) | async-done | bytes 4718624 | tf_op jit(solution)/shard_map/all_to_all | solution.py:66
  161.5 4.9 %copy.94 = bf16[2,16,2,16,2304]{4,3,2,1,0:T(8,128)(2,1)} copy(bf16[2,16,2,16,2304]{4,3,2,0,1:T(8,128)(2,1)} %all-to-all-done.1) | data formatting | bytes 9437184 | tf_op jit(solution)/shard_map/all_to_all | solution.py:66
  166.4 13.5 %gather_fusion.3 = bf16[512,2304]{1,0:T(8,128)(2,1)} fusion(bf16[2,512,2304]{2,1,0:T(8,128)(2,1)} %bitcast.72, s32[512]{0:T(512)S(1)} %bitcast.70), kind=kCustom, calls=%fused_computation.3 | custom fusion | bytes 4722688 | tf_op jit(solution)/shard_map/vmap(jit(_take))/gather | solution.py:24
  179.9 2.4 convert_reduce_fusion
  182.2 0.0 copy-start
  182.2 2.5 reduce_sum.42
  184.7 5.5 %reduce_sum.43 = f32[128,2304]{1,0:T(8,128)} reduce(f32[128,2,2304]{2,1,0:T(2,128)} %reduce_sum.42, f32[]{:T(128)} %constant.104.clone.1), dimensions={1}, to_apply=%region_5.6 | reduce | flops 294912 | bytes 3538948 | tf_op jit(solution)/shard_map/reduce_sum | solution.py:70
  190.2 0.0 all-reduce.4.cloned.1.call-update
  190.2 0.1 broadcast_in_dim.73
  190.3 60.1 %all-reduce.4.cloned.1.call-done = f32[128,2304]{1,0:T(8,128)} async-done(((f32[128,2304]{1,0:T(8,128)}), f32[128,2304]{1,0:T(8,128)}) %all-reduce.4.cloned.1.call-update) | async-done | bytes 1179664 | tf_op jit(solution)/shard_map/psum | solution.py:73
  250.4 0.0 copy-done
  250.4 1.5 multiply_reduce_fusion
  252.0 1.5 multiply_convert_fusion
  253.5 6.2 %gather_fusion = bf16[1024,2304]{1,0:T(8,128)(2,1)} fusion(bf16[129,2304]{1,0:T(8,128)(2,1)S(1)} %concatenate.10, s32[1024]{0:T(1024)S(1)} %broadcast_clamp_fusion), kind=kCustom, calls=%fused_computation | custom fusion | bytes 9441280 | tf_op jit(solution)/shard_map/jit(_take)/gather | solution.py:75
  259.7 2.8 broadcast_select_fusion
  262.5 2.6 copy.96
  265.1 5.8 %all-to-all-start.2 = ((bf16[2,16,2,16,2304]{4,3,2,0,1:T(8,128)(2,1)}), bf16[2,16,2,16,2304]{4,3,2,0,1:T(8,128)(2,1)}, u32[]{:S(2)}, u32[]{:S(2)}) async-start(bf16[2,16,2,16,2304]{4,3,2,0,1:T(8,128)(2,1)} %copy.96), calls=%async_computation.2 | async-start | bytes 9437184 | tf_op jit(solution)/shard_map/all_to_all | solution.py:78
  270.9 6.9 %gather_fusion.1 = s32[1024]{0:T(1024)S(1)} fusion(s32[129]{0:T(256)S(1)} %pad_add_fusion, s32[1024]{0:T(1024)S(1)} %broadcast_clamp_fusion), kind=kCustom, calls=%fused_computation.1 | custom fusion | bytes 12288 | tf_op jit(solution)/shard_map/jit(_take)/gather | solution.py:56
  277.8 0.1 gather.36
  277.9 0.6 copy.101
  278.6 79.0 %all-to-all-done.2 = bf16[2,16,2,16,2304]{4,3,2,0,1:T(8,128)(2,1)} async-done(((bf16[2,16,2,16,2304]{4,3,2,0,1:T(8,128)(2,1)}), bf16[2,16,2,16,2304]{4,3,2,0,1:T(8,128)(2,1)}, u32[]{:S(2)}, u32[]{:S(2)}) %all-to-all-start.2) | async-done | bytes 4718624 | tf_op jit(solution)/shard_map/all_to_all | solution.py:78
  357.6 21.7 %all-to-all-start.4 = ((s32[2,16,2,16]{3,2,0,1:T(2,128)}), s32[2,16,2,16]{3,2,0,1:T(2,128)S(1)}, u32[]{:S(2)}, u32[]{:S(2)}) async-start(s32[2,16,2,16]{3,2,0,1:T(2,128)} %copy.101), calls=%async_computation.4 | async-start | bytes 65536 | tf_op jit(solution)/shard_map/all_to_all | solution.py:61
  379.3 0.0 copy-start.3
  379.4 5.2 %fusion.6 = bf16[2,16,2,16,256]{4,3,1,2,0:T(8,128)(2,1)S(1)} fusion(bf16[2,2,256,2304,1]{3,2,4,1,0:T(8,128)(2,1)} %bitcast.79, bf16[2,16,2,16,2304]{4,3,2,0,1:T(8,128)(2,1)} %all-to-all-done.2), kind=kOutput, calls=%fused_computation.13 | convolution fusion | flops 1208221696 | bytes 9961472 | tf_op jit(solution)/shard_map/lspcd,lpjd->lspcj/dot_general | solution.py:79
  384.6 0.0 copy-start.2
  384.6 0.9 copy.98
  385.4 0.6 all-to-all-done.4
  386.0 5.5 %all-to-all-start.3 = ((bf16[2,16,2,16,256]{4,3,2,0,1:T(8,128)(2,1)}), bf16[2,16,2,16,256]{4,3,2,0,1:T(8,128)(2,1)S(1)}, u32[]{:S(2)}, u32[]{:S(2)}) async-start(bf16[2,16,2,16,256]{4,3,2,0,1:T(8,128)(2,1)} %copy.98), calls=%async_computation.3 | async-start | bytes 1048576 | tf_op jit(solution)/shard_map/all_to_all | solution.py:82
  391.4 0.1 reduce_sum.39
  391.6 0.1 copy.87
  391.7 0.2 copy.88
  391.9 0.7 convolution_bitcast_fusion
  392.6 0.1 copy.107
  392.6 0.7 reshape.203
  393.3 12.4 %all-to-all-done.3 = bf16[2,16,2,16,256]{4,3,2,0,1:T(8,128)(2,1)S(1)} async-done(((bf16[2,16,2,16,256]{4,3,2,0,1:T(8,128)(2,1)}), bf16[2,16,2,16,256]{4,3,2,0,1:T(8,128)(2,1)S(1)}, u32[]{:S(2)}, u32[]{:S(2)}) %all-to-all-start.3) | async-done | bytes 524320 | tf_op jit(solution)/shard_map/all_to_all | solution.py:82
  405.8 3.2 gather_fusion.4
  408.9 0.1 gather.34
  409.1 1.4 multiply_convert_fusion.1
  (28 shorter events, 0.3 us)
Async XLA Ops:
  7.2 28.4 %copy-start.5 = (s32[128]{0:T(128)S(1)}, s32[128]{0:T(128)}, u32[]{:S(2)}) copy-start(s32[128]{0:T(128)} %param.8) | copy-start | bytes 1540
  7.2 28.5 %copy-start.1 = (bf16[2,128,2,256]{3,2,1,0:T(2,128)(2,1)S(1)}, bf16[2,128,2,256]{3,2,1,0:T(2,128)(2,1)}, u32[]{:S(2)}) copy-start(bf16[2,128,2,256]{3,2,1,0:T(2,128)(2,1)} %param.6) | copy-start | bytes 786436
  70.3 91.2 %all-to-all-start.1 = ((bf16[2,16,2,16,2304]{4,3,2,0,1:T(8,128)(2,1)}), bf16[2,16,2,16,2304]{4,3,2,0,1:T(8,128)(2,1)}, u32[]{:S(2)}, u32[]{:S(2)}) async-start(bf16[2,16,2,16,2304]{4,3,2,0,1:T(8,128)(2,1)} %copy.93), calls=%async_computation.1 | async-start | bytes 9437184 | tf_op jit(solution)/shard_map/all_to_all | solution.py:66
  74.9 175.5 %all-reduce.4.cloned.1.call-start = ((), (), s32[]{:S(2)}) async-start(), calls=%async_computation.5 | async-start | bytes 2359296 | tf_op jit(solution)/shard_map/psum | solution.py:73
  182.2 68.2 %copy-start = (bf16[128,2304]{1,0:T(8,128)(2,1)S(1)}, bf16[128,2304]{1,0:T(8,128)(2,1)}, u32[]{:S(2)}) copy-start(bf16[128,2304]{1,0:T(8,128)(2,1)} %param.10) | copy-start | bytes 1769476
  265.1 5.8 %copy-start.4 = (s32[128]{0:T(128)S(1)}, s32[128]{0:T(128)}, u32[]{:S(2)}) copy-start(s32[128]{0:T(128)} %param.9) | copy-start | bytes 1540
  265.1 92.5 %all-to-all-start.2 = ((bf16[2,16,2,16,2304]{4,3,2,0,1:T(8,128)(2,1)}), bf16[2,16,2,16,2304]{4,3,2,0,1:T(8,128)(2,1)}, u32[]{:S(2)}, u32[]{:S(2)}) async-start(bf16[2,16,2,16,2304]{4,3,2,0,1:T(8,128)(2,1)} %copy.96), calls=%async_computation.2 | async-start | bytes 9437184 | tf_op jit(solution)/shard_map/all_to_all | solution.py:78
  357.6 28.4 %all-to-all-start.4 = ((s32[2,16,2,16]{3,2,0,1:T(2,128)}), s32[2,16,2,16]{3,2,0,1:T(2,128)S(1)}, u32[]{:S(2)}, u32[]{:S(2)}) async-start(s32[2,16,2,16]{3,2,0,1:T(2,128)} %copy.101), calls=%async_computation.4 | async-start | bytes 65536 | tf_op jit(solution)/shard_map/all_to_all | solution.py:61
  379.3 12.3 %copy-start.3 = (s32[2,128,2]{1,2,0:T(2,128)S(1)}, s32[2,128,2]{1,2,0:T(2,128)}, u32[]{:S(2)}) copy-start(s32[2,128,2]{1,2,0:T(2,128)} %param.7) | copy-start | bytes 6148
  384.6 24.5 %copy-start.2 = (bf16[2,128,2,256]{3,2,1,0:T(2,128)(2,1)S(1)}, bf16[2,128,2,256]{3,2,1,0:T(2,128)(2,1)}, u32[]{:S(2)}) copy-start(bf16[2,128,2,256]{3,2,1,0:T(2,128)(2,1)} %param.6) | copy-start | bytes 786436
  386.0 19.7 %all-to-all-start.3 = ((bf16[2,16,2,16,256]{4,3,2,0,1:T(8,128)(2,1)}), bf16[2,16,2,16,256]{4,3,2,0,1:T(8,128)(2,1)S(1)}, u32[]{:S(2)}, u32[]{:S(2)}) async-start(bf16[2,16,2,16,256]{4,3,2,0,1:T(8,128)(2,1)} %copy.98), calls=%async_computation.3 | async-start | bytes 1048576 | tf_op jit(solution)/shard_map/all_to_all | solution.py:82
Sparse Core Ops, SparseCore 0:
  190.3 60.0 all-reduce.3
where the time goes:
time: 418 us; the launch traced here: 417 us
  waiting for transfers between devices  238 us (57%)
  local copies, waits for them, and re-layouts  77.8 us (19%)
  starting transfers between devices  37.8 us (9%)
  blocking collectives  21.5 us (5%)
  other arithmetic  17.8 us (4%)
  between operations  14.4 us (3%)
  matrix products  9.61 us (2%)
    all_to_all x1, waiting for transfers between devices, per_device(): lax.all_to_all(built, 'tok', split_axis=1, concat_axis=1, tiled=True)  86.4 us
    all_to_all x1, waiting for transfers between devices, per_device(): lax.all_to_all(send_grad, 'tok', split_axis=1, concat_axis=1, tiled=True)  79 us
    psum x1, waiting for transfers between devices, per_device(): rebuilt = lax.psum(partial_value, 'lyr')  60.1 us
    scatter x1, local copies, waits for them, and re-layouts, source_of(): return empty.at[slot_ids].set(jnp.arange(row_count, dtype=jnp.int32))  24.5 us
    gather x4, local copies, waits for them, and re-layouts, take_rows(): return jnp.take(table, index, axis=0)  22.2 us
    all_to_all x1, starting transfers between devices, per_device(): lax.all_to_all(slot_requests, 'tok', split_axis=1, concat_axis=1, tiled=T...  21.7 us
    all_to_all x1, blocking collectives, per_device(): lax.all_to_all(send_codes, 'tok', split_axis=1, concat_axis=1, tiled=True)  21.5 us
    all_to_all x1, waiting for transfers between devices, per_device(): lax.all_to_all(projected_slots, 'tok', split_axis=1, concat_axis=1, tiled...  12.4 us
  transfers between devices with their start and end apart: 5, of which 5 were waited for; matrix products, arithmetic and copies ran while one was open for 4% of the time, Pallas kernels for 0%

commit v1 on v0

--- a/solution.py
+++ b/solution.py
@@ -6,6 +6,31 @@
 PANELS = 32
 REQUESTS = 16
 CAP = 16
+
+
+def entries_solve(field, dimension_no, axis_k):
+    finding = lax.axis_size("tok")
+    aux = lax.axis_index("tok")
+    r2, current_value = (finding, aux)
+    passed = field.shape[dimension_no] // r2
+    current_arr = list(field.shape)
+    current_arr[dimension_no] = passed
+    later = current_arr[axis_k]
+    current_arr[axis_k] = later * r2
+    v_next = jnp.zeros(current_arr, field.dtype)
+    for num in range(r2):
+        z1 = lax.dynamic_slice_in_dim(
+            field, (current_value ^ num) * passed, passed, axis=dimension_no
+        )
+        if num:
+            sheets = []
+            for it in range(r2):
+                sheets.append((it, it ^ num))
+            z1 = lax.ppermute(z1, "tok", sheets)
+        v_next = lax.dynamic_update_slice_in_dim(
+            v_next, z1, (current_value ^ num) * later, axis=axis_k
+        )
+    return v_next
 
 
 def slot_of(flat_ids):
@@ -63,9 +88,7 @@
     built = jnp.einsum(
         "lspcj,lpjd->lspcd", received, panel_weights, preferred_element_type=jnp.float32
     ).astype(jnp.bfloat16)
-    returned = lax.all_to_all(built, "tok", split_axis=1, concat_axis=1, tiled=True).reshape(
-        layers_here, PANELS * CAP, width
-    )
+    returned = entries_solve(built, 1, 1).reshape(layers_here, PANELS * CAP, width)
     per_row = jax.vmap(take_rows)(returned, slot_ids)
     partial_value = jnp.sum(
         per_row.astype(jnp.float32).reshape(layers_here, count, kact, width), axis=(0, 2)

time: 418 us -> 424 us (1.014)
  starting transfers between devices: 37.8 us -> 82.8 us
  waiting for transfers between devices: 238 us -> 212 us
  blocking collectives: 21.5 us -> 0 us
  local copies, waits for them, and re-layouts: 77.8 us -> 85.9 us
    all_to_all x1, waiting for transfers between devices: 86.4 us -> 13.9 us  [per_device(): lax.all_to_all(send_codes, 'tok', split_axis=1, concat_axis=1, tiled=True)]
    ppermute x0 -> x15, waiting for transfers between devices: none -> 42.7 us  [entries_solve(): z1 = lax.ppermute(z1, 'tok', sheets)]
    ppermute x0 -> x15, starting transfers between devices: none -> 42.2 us  [entries_solve(): z1 = lax.ppermute(z1, 'tok', sheets)]
    all_to_all x1 -> x0, blocking collectives: 21.5 us -> none  [per_device(): lax.all_to_all(send_codes, 'tok', split_axis=1, concat_axis=1, tiled=True)]
    dynamic_update_slice x0 -> x16, local copies, waits for them, and re-layouts: none -> 11.8 us  [entries_solve(): lax.dynamic_update_slice_in_dim(v_next, z1, (current_value ^ num) * later...]
    all_to_all x1 -> x0, local copies, waits for them, and re-layouts: 4.86 us -> none  [per_device(): lax.all_to_all(built, 'tok', split_axis=1, concat_axis=1, tiled=True)]
  transfers between devices with their start and end apart: 5 -> 20, of which waited for: 5 -> 11; matrix products, arithmetic and copies ran while one was open for 4% -> 7% of each run, Pallas kernels for 0% -> 0%
where the time goes in v1:
time: 424 us; the launch traced here: 423 us
  waiting for transfers between devices  212 us (50%)
  local copies, waits for them, and re-layouts  85.9 us (20%)
  starting transfers between devices  82.8 us (20%)
  other arithmetic  17.8 us (4%)
  between operations  14.6 us (3%)
  matrix products  9.62 us (2%)
    all_to_all x1, waiting for transfers between devices, per_device(): lax.all_to_all(send_grad, 'tok', split_axis=1, concat_axis=1, tiled=True)  79 us
    psum x1, waiting for transfers between devices, per_device(): rebuilt = lax.psum(partial_value, 'lyr')  63.5 us
    ppermute x15, waiting for transfers between devices, entries_solve(): z1 = lax.ppermute(z1, 'tok', sheets)  42.7 us
    ppermute x15, starting transfers between devices, entries_solve(): z1 = lax.ppermute(z1, 'tok', sheets)  42.2 us
    scatter x1, local copies, waits for them, and re-layouts, source_of(): return empty.at[slot_ids].set(jnp.arange(row_count, dtype=jnp.int32))  24.5 us
    gather x4, local copies, waits for them, and re-layouts, take_rows(): return jnp.take(table, index, axis=0)  22.3 us
    all_to_all x1, starting transfers between devices, per_device(): lax.all_to_all(slot_requests, 'tok', split_axis=1, concat_axis=1, tiled=T...  21.7 us
    all_to_all x1, waiting for transfers between devices, per_device(): lax.all_to_all(send_codes, 'tok', split_axis=1, concat_axis=1, tiled=True)  13.9 us
  transfers between devices with their start and end apart: 20, of which 11 were waited for; matrix products, arithmetic and copies ran while one was open for 7% of the time, Pallas kernels for 0%

profile of v1, /device:TPU:0, one launch (start us, length us, event | category | flops | bytes accessed | tf_op | source)
XLA Modules:
  0.0 422.8 jit_solution(6471399462986205689)
XLA Ops:
  7.2 0.7 broadcast_multiply_fusion.1
  7.9 0.8 copy.77
  9.3 1.2 reduce-window.6
  10.9 24.5 %scatter_fusion = s32[2,512]{1,0:T(2,128)S(1)} fusion(s32[2,512]{1,0:T(2,128)S(1)} %broadcast_in_dim.74, s32[512]{0:T(512)S(1)} %bitcast.103, s32[512]{0:T(512)S(1)} %bitcast.113), kind=kCustom, calls=%fused_computation.5 | custom fusion | bytes 10240 | tf_op jit(solution)/shard_map/vmap()/scatter | solution.py:45
  36.7 5.5 %gather_fusion.2 = bf16[1024,256]{1,0:T(8,128)(2,1)S(1)} fusion(bf16[2,257,256]{2,0,1:T(2,128)(2,1)S(1)} %concatenate.9, s32[1024]{0:T(1024)S(1)} %bitcast.102), kind=kCustom, calls=%fused_computation.2 | custom fusion | bytes 1056768 | tf_op jit(solution)/shard_map/vmap(jit(_take))/gather | solution.py:49
  42.4 0.8 copy.84
  43.2 7.4 %all-to-all-start = ((bf16[2,16,2,16,256]{4,3,2,0,1:T(8,128)(2,1)}), bf16[2,16,2,16,256]{4,3,2,0,1:T(8,128)(2,1)S(1)}, u32[]{:S(2)}, u32[]{:S(2)}) async-start(bf16[2,16,2,16,256]{4,3,2,0,1:T(8,128)(2,1)} %copy.84), calls=%async_computation | async-start | bytes 1048576 | tf_op jit(solution)/shard_map/all_to_all | solution.py:85
  51.0 13.9 %all-to-all-done = bf16[2,16,2,16,256]{4,3,2,0,1:T(8,128)(2,1)S(1)} async-done(((bf16[2,16,2,16,256]{4,3,2,0,1:T(8,128)(2,1)}), bf16[2,16,2,16,256]{4,3,2,0,1:T(8,128)(2,1)S(1)}, u32[]{:S(2)}, u32[]{:S(2)}) %all-to-all-start) | async-done | bytes 524320 | tf_op jit(solution)/shard_map/all_to_all | solution.py:85
  64.9 3.7 convolution_convert_fusion
  69.3 1.3 collective-permute-start.1
  71.0 1.5 collective-permute-start.3
  72.8 2.7 broadcast_in_dim.79
  75.4 0.7 bitcast_dynamic-update-slice_fusion
  76.2 2.1 collective-permute-start.5
  78.3 0.7 constant_dynamic-update-slice_fusion.14
  79.5 0.7 constant_dynamic-update-slice_fusion.13
  80.3 4.0 collective-permute-done.2
  84.2 2.5 collective-permute-start.7
  86.7 0.7 constant_dynamic-update-slice_fusion.12
  88.0 0.8 constant_dynamic-update-slice_fusion.11
  88.8 2.1 collective-permute-start.9
  90.9 0.7 constant_dynamic-update-slice_fusion.10
  91.6 14.1 %collective-permute-done.5 = bf16[2,1,2,16,2304]{4,3,2,1,0:T(8,128)(2,1)S(1)} collective-permute-done((bf16[2,1,2,16,2304]{4,3,2,1,0:T(8,128)(2,1)S(1)}, bf16[2,1,2,16,2304]{4,3,2,1,0:T(8,128)(2,1)S(1)}, u32[]{:S(2)}, u32[]{:S(2)}) %collective-permute-start.5) | collective-permute-done | bytes 294944 | tf_op jit(solution)/shard_map/ppermute | solution.py:29
  105.7 0.7 constant_dynamic-update-slice_fusion.9
  106.5 5.0 %collective-permute-done.6 = bf16[2,1,2,16,2304]{4,3,2,1,0:T(8,128)(2,1)S(1)} collective-permute-done((bf16[2,1,2,16,2304]{4,3,2,1,0:T(8,128)(2,1)S(1)}, bf16[2,1,2,16,2304]{4,3,2,1,0:T(8,128)(2,1)S(1)}, u32[]{:S(2)}, u32[]{:S(2)}) %collective-permute-start.6) | collective-permute-done | bytes 294944 | tf_op jit(solution)/shard_map/ppermute | solution.py:29
  111.5 2.5 collective-permute-start.11
  114.0 0.7 constant_dynamic-update-slice_fusion.8
  114.7 0.8 collective-permute-start.12
  115.5 0.7 constant_dynamic-update-slice_fusion.7
  116.3 25.6 %collective-permute-start.13 = (bf16[2,1,2,16,2304]{4,3,2,1,0:T(8,128)(2,1)S(1)}, bf16[2,1,2,16,2304]{4,3,2,1,0:T(8,128)(2,1)S(1)}, u32[]{:S(2)}, u32[]{:S(2)}) collective-permute-start(bf16[2,1,2,16,2304]{4,3,2,1,0:T(8,128)(2,1)S(1)} %get-tuple-element.15), channel_id=1, source_target_pairs={{0,28},{2,30},{4,24},{6,26},{8,20},{10,22},{12,16},{14,18},{16,12}... | collective-permute-start | bytes 884744 | tf_op jit(solution)/shard_map/ppermute | solution.py:29
  141.9 0.7 constant_dynamic-update-slice_fusion.6
  142.6 9.5 %collective-permute-done.9 = bf16[2,1,2,16,2304]{4,3,2,1,0:T(8,128)(2,1)S(1)} collective-permute-done((bf16[2,1,2,16,2304]{4,3,2,1,0:T(8,128)(2,1)S(1)}, bf16[2,1,2,16,2304]{4,3,2,1,0:T(8,128)(2,1)S(1)}, u32[]{:S(2)}, u32[]{:S(2)}) %collective-permute-start.9) | collective-permute-done | bytes 294944 | tf_op jit(solution)/shard_map/ppermute | solution.py:29
  152.0 2.0 collective-permute-start.14
  154.0 0.8 constant_dynamic-update-slice_fusion.5
  154.8 10.0 %collective-permute-done.10 = bf16[2,1,2,16,2304]{4,3,2,1,0:T(8,128)(2,1)S(1)} collective-permute-done((bf16[2,1,2,16,2304]{4,3,2,1,0:T(8,128)(2,1)S(1)}, bf16[2,1,2,16,2304]{4,3,2,1,0:T(8,128)(2,1)S(1)}, u32[]{:S(2)}, u32[]{:S(2)}) %collective-permute-start.10) | collective-permute-done | bytes 294944 | tf_op jit(solution)/shard_map/ppermute | solution.py:29
  164.8 0.7 constant_dynamic-update-slice_fusion.4
  165.5 0.7 constant_dynamic-update-slice_fusion.3
  166.2 0.7 constant_dynamic-update-slice_fusion.2
  167.0 0.7 constant_dynamic-update-slice_fusion.1
  167.7 0.7 constant_dynamic-update-slice_fusion
  168.5 13.5 %gather_fusion.3 = bf16[512,2304]{1,0:T(8,128)(2,1)} fusion(bf16[2,512,2304]{2,1,0:T(8,128)(2,1)} %bitcast.24, s32[512]{0:T(512)S(1)} %bitcast.100), kind=kCustom, calls=%fused_computation.3 | custom fusion | bytes 4722688 | tf_op jit(solution)/shard_map/vmap(jit(_take))/gather | solution.py:49
  182.0 2.4 convert_reduce_fusion
  184.3 2.5 reduce_sum.42
  186.8 5.5 %reduce_sum.43 = f32[128,2304]{1,0:T(8,128)} reduce(f32[128,2,2304]{2,1,0:T(2,128)} %reduce_sum.42, f32[]{:T(128)} %constant.137.clone.1), dimensions={1}, to_apply=%region_5.6 | reduce | flops 294912 | bytes 3538948 | tf_op jit(solution)/shard_map/reduce_sum | solution.py:93
  192.4 63.5 %all-reduce.4.cloned.1.call-done = f32[128,2304]{1,0:T(8,128)} async-done(((f32[128,2304]{1,0:T(8,128)}), f32[128,2304]{1,0:T(8,128)}) %all-reduce.4.cloned.1.call-update) | async-done | bytes 1179664 | tf_op jit(solution)/shard_map/psum | solution.py:96
  256.0 1.5 multiply_reduce_fusion
  257.5 1.5 multiply_convert_fusion
  259.0 6.2 %gather_fusion = bf16[1024,2304]{1,0:T(8,128)(2,1)} fusion(bf16[129,2304]{1,0:T(8,128)(2,1)S(1)} %concatenate.10, s32[1024]{0:T(1024)S(1)} %broadcast_clamp_fusion), kind=kCustom, calls=%fused_computation | custom fusion | bytes 9441280 | tf_op jit(solution)/shard_map/jit(_take)/gather | solution.py:98
  265.2 2.8 broadcast_select_fusion
  268.1 2.6 copy.87
  270.7 5.8 %all-to-all-start.1 = ((bf16[2,16,2,16,2304]{4,3,2,0,1:T(8,128)(2,1)}), bf16[2,16,2,16,2304]{4,3,2,0,1:T(8,128)(2,1)}, u32[]{:S(2)}, u32[]{:S(2)}) async-start(bf16[2,16,2,16,2304]{4,3,2,0,1:T(8,128)(2,1)} %copy.87), calls=%async_computation.1 | async-start | bytes 9437184 | tf_op jit(solution)/shard_map/all_to_all | solution.py:101
  276.5 6.9 %gather_fusion.1 = s32[1024]{0:T(1024)S(1)} fusion(s32[129]{0:T(256)S(1)} %pad_add_fusion, s32[1024]{0:T(1024)S(1)} %broadcast_clamp_fusion), kind=kCustom, calls=%fused_computation.1 | custom fusion | bytes 12288 | tf_op jit(solution)/shard_map/jit(_take)/gather | solution.py:81
  283.5 0.6 copy.92
  284.1 79.0 %all-to-all-done.1 = bf16[2,16,2,16,2304]{4,3,2,0,1:T(8,128)(2,1)} async-done(((bf16[2,16,2,16,2304]{4,3,2,0,1:T(8,128)(2,1)}), bf16[2,16,2,16,2304]{4,3,2,0,1:T(8,128)(2,1)}, u32[]{:S(2)}, u32[]{:S(2)}) %all-to-all-start.1) | async-done | bytes 4718624 | tf_op jit(solution)/shard_map/all_to_all | solution.py:101
  363.1 21.7 %all-to-all-start.3 = ((s32[2,16,2,16]{3,2,0,1:T(2,128)}), s32[2,16,2,16]{3,2,0,1:T(2,128)S(1)}, u32[]{:S(2)}, u32[]{:S(2)}) async-start(s32[2,16,2,16]{3,2,0,1:T(2,128)} %copy.92), calls=%async_computation.3 | async-start | bytes 65536 | tf_op jit(solution)/shard_map/all_to_all | solution.py:86
  384.9 5.2 %fusion.5 = bf16[2,16,2,16,256]{4,3,1,2,0:T(8,128)(2,1)S(1)} fusion(bf16[2,2,256,2304,1]{3,2,4,1,0:T(8,128)(2,1)} %bitcast.108, bf16[2,16,2,16,2304]{4,3,2,0,1:T(8,128)(2,1)} %all-to-all-done.1), kind=kOutput, calls=%fused_computation.12 | convolution fusion | flops 1208221696 | bytes 9961472 | tf_op jit(solution)/shard_map/lspcd,lpjd->lspcj/dot_general | solution.py:102
  390.1 0.9 copy.89
  391.0 0.5 all-to-all-done.3
  391.5 5.5 %all-to-all-start.2 = ((bf16[2,16,2,16,256]{4,3,2,0,1:T(8,128)(2,1)}), bf16[2,16,2,16,256]{4,3,2,0,1:T(8,128)(2,1)S(1)}, u32[]{:S(2)}, u32[]{:S(2)}) async-start(bf16[2,16,2,16,256]{4,3,2,0,1:T(8,128)(2,1)} %copy.89), calls=%async_computation.2 | async-start | bytes 1048576 | tf_op jit(solution)/shard_map/all_to_all | solution.py:105
  397.4 0.7 convolution_bitcast_fusion
  398.2 0.7 reshape.219
  398.9 12.4 %all-to-all-done.2 = bf16[2,16,2,16,256]{4,3,2,0,1:T(8,128)(2,1)S(1)} async-done(((bf16[2,16,2,16,256]{4,3,2,0,1:T(8,128)(2,1)}), bf16[2,16,2,16,256]{4,3,2,0,1:T(8,128)(2,1)S(1)}, u32[]{:S(2)}, u32[]{:S(2)}) %all-to-all-start.2) | async-done | bytes 524320 | tf_op jit(solution)/shard_map/all_to_all | solution.py:105
  411.3 3.2 gather_fusion.4
  414.6 1.4 multiply_convert_fusion.1
  (73 shorter events, 5.9 us)
Async XLA Ops:
  7.2 28.4 %copy-start.5 = (s32[128]{0:T(128)S(1)}, s32[128]{0:T(128)}, u32[]{:S(2)}) copy-start(s32[128]{0:T(128)} %param.8) | copy-start | bytes 1540
  7.2 28.4 %copy-start.1 = (bf16[2,128,2,256]{3,2,1,0:T(2,128)(2,1)S(1)}, bf16[2,128,2,256]{3,2,1,0:T(2,128)(2,1)}, u32[]{:S(2)}) copy-start(bf16[2,128,2,256]{3,2,1,0:T(2,128)(2,1)} %param.6) | copy-start | bytes 786436
  43.2 21.7 %all-to-all-start = ((bf16[2,16,2,16,256]{4,3,2,0,1:T(8,128)(2,1)}), bf16[2,16,2,16,256]{4,3,2,0,1:T(8,128)(2,1)S(1)}, u32[]{:S(2)}, u32[]{:S(2)}) async-start(bf16[2,16,2,16,256]{4,3,2,0,1:T(8,128)(2,1)} %copy.84), calls=%async_computation | async-start | bytes 1048576 | tf_op jit(solution)/shard_map/all_to_all | solution.py:85
  50.6 205.3 %all-reduce.4.cloned.1.call-start = ((), (), s32[]{:S(2)}) async-start(), calls=%async_computation.4 | async-start | bytes 2359296 | tf_op jit(solution)/shard_map/psum | solution.py:96
  69.0 7.1 %collective-permute-start = (bf16[2,1,2,16,2304]{4,3,2,1,0:T(8,128)(2,1)S(1)}, bf16[2,1,2,16,2304]{4,3,2,1,0:T(8,128)(2,1)S(1)}, u32[]{:S(2)}, u32[]{:S(2)}) collective-permute-start(bf16[2,1,2,16,2304]{4,3,2,1,0:T(8,128)(2,1)S(1)} %get-tuple-element.28), channel_id=1, source_target_pairs={{0,2},{2,0},{4,6},{6,4},{8,10},{10,8},{12,14},{14,12},{16,18},{18,... | collective-permute-start | bytes 884744 | tf_op jit(solution)/shard_map/ppermute | solution.py:29
  69.3 9.9 %collective-permute-start.1 = (bf16[2,1,2,16,2304]{4,3,2,1,0:T(8,128)(2,1)S(1)}, bf16[2,1,2,16,2304]{4,3,2,1,0:T(8,128)(2,1)S(1)}, u32[]{:S(2)}, u32[]{:S(2)}) collective-permute-start(bf16[2,1,2,16,2304]{4,3,2,1,0:T(8,128)(2,1)S(1)} %get-tuple-element.27), channel_id=1, source_target_pairs={{0,4},{2,6},{4,0},{6,2},{8,12},{10,14},{12,8},{14,10},{16,20},{18,... | collective-permute-start | bytes 884744 | tf_op jit(solution)/shard_map/ppermute | solution.py:29
  70.5 13.7 %collective-permute-start.2 = (bf16[2,1,2,16,2304]{4,3,2,1,0:T(8,128)(2,1)S(1)}, bf16[2,1,2,16,2304]{4,3,2,1,0:T(8,128)(2,1)S(1)}, u32[]{:S(2)}, u32[]{:S(2)}) collective-permute-start(bf16[2,1,2,16,2304]{4,3,2,1,0:T(8,128)(2,1)S(1)} %get-tuple-element.26), channel_id=1, source_target_pairs={{0,6},{2,4},{4,2},{6,0},{8,14},{10,12},{12,10},{14,8},{16,22},{18,... | collective-permute-start | bytes 884744 | tf_op jit(solution)/shard_map/ppermute | solution.py:29
  71.0 16.5 %collective-permute-start.3 = (bf16[2,1,2,16,2304]{4,3,2,1,0:T(8,128)(2,1)S(1)}, bf16[2,1,2,16,2304]{4,3,2,1,0:T(8,128)(2,1)S(1)}, u32[]{:S(2)}, u32[]{:S(2)}) collective-permute-start(bf16[2,1,2,16,2304]{4,3,2,1,0:T(8,128)(2,1)S(1)} %get-tuple-element.25), channel_id=1, source_target_pairs={{0,8},{2,10},{4,12},{6,14},{8,0},{10,2},{12,4},{14,6},{16,24},{18,... | collective-permute-start | bytes 884744 | tf_op jit(solution)/shard_map/ppermute | solution.py:29
  72.4 16.3 %collective-permute-start.4 = (bf16[2,1,2,16,2304]{4,3,2,1,0:T(8,128)(2,1)S(1)}, bf16[2,1,2,16,2304]{4,3,2,1,0:T(8,128)(2,1)S(1)}, u32[]{:S(2)}, u32[]{:S(2)}) collective-permute-start(bf16[2,1,2,16,2304]{4,3,2,1,0:T(8,128)(2,1)S(1)} %get-tuple-element.24), channel_id=1, source_target_pairs={{0,10},{2,8},{4,14},{6,12},{8,2},{10,0},{12,6},{14,4},{16,26},{18,... | collective-permute-start | bytes 884744 | tf_op jit(solution)/shard_map/ppermute | solution.py:29
  76.2 29.5 %collective-permute-start.5 = (bf16[2,1,2,16,2304]{4,3,2,1,0:T(8,128)(2,1)S(1)}, bf16[2,1,2,16,2304]{4,3,2,1,0:T(8,128)(2,1)S(1)}, u32[]{:S(2)}, u32[]{:S(2)}) collective-permute-start(bf16[2,1,2,16,2304]{4,3,2,1,0:T(8,128)(2,1)S(1)} %get-tuple-element.23), channel_id=1, source_target_pairs={{0,12},{2,14},{4,8},{6,10},{8,4},{10,6},{12,0},{14,2},{16,28},{18,... | collective-permute-start | bytes 884744 | tf_op jit(solution)/shard_map/ppermute | solution.py:29
  79.1 32.4 %collective-permute-start.6 = (bf16[2,1,2,16,2304]{4,3,2,1,0:T(8,128)(2,1)S(1)}, bf16[2,1,2,16,2304]{4,3,2,1,0:T(8,128)(2,1)S(1)}, u32[]{:S(2)}, u32[]{:S(2)}) collective-permute-start(bf16[2,1,2,16,2304]{4,3,2,1,0:T(8,128)(2,1)S(1)} %get-tuple-element.22), channel_id=1, source_target_pairs={{0,14},{2,12},{4,10},{6,8},{8,6},{10,4},{12,2},{14,0},{16,30},{18,... | collective-permute-start | bytes 884744 | tf_op jit(solution)/shard_map/ppermute | solution.py:29
  84.2 30.5 %collective-permute-start.7 = (bf16[2,1,2,16,2304]{4,3,2,1,0:T(8,128)(2,1)S(1)}, bf16[2,1,2,16,2304]{4,3,2,1,0:T(8,128)(2,1)S(1)}, u32[]{:S(2)}, u32[]{:S(2)}) collective-permute-start(bf16[2,1,2,16,2304]{4,3,2,1,0:T(8,128)(2,1)S(1)} %get-tuple-element.21), channel_id=1, source_target_pairs={{0,16},{2,18},{4,20},{6,22},{8,24},{10,26},{12,28},{14,30},{16,0},... | collective-permute-start | bytes 884744 | tf_op jit(solution)/shard_map/ppermute | solution.py:29
  87.5 28.8 %collective-permute-start.8 = (bf16[2,1,2,16,2304]{4,3,2,1,0:T(8,128)(2,1)S(1)}, bf16[2,1,2,16,2304]{4,3,2,1,0:T(8,128)(2,1)S(1)}, u32[]{:S(2)}, u32[]{:S(2)}) collective-permute-start(bf16[2,1,2,16,2304]{4,3,2,1,0:T(8,128)(2,1)S(1)} %get-tuple-element.20), channel_id=1, source_target_pairs={{0,18},{2,16},{4,22},{6,20},{8,26},{10,24},{12,30},{14,28},{16,2},... | collective-permute-start | bytes 884744 | tf_op jit(solution)/shard_map/ppermute | solution.py:29
  88.8 63.3 %collective-permute-start.9 = (bf16[2,1,2,16,2304]{4,3,2,1,0:T(8,128)(2,1)S(1)}, bf16[2,1,2,16,2304]{4,3,2,1,0:T(8,128)(2,1)S(1)}, u32[]{:S(2)}, u32[]{:S(2)}) collective-permute-start(bf16[2,1,2,16,2304]{4,3,2,1,0:T(8,128)(2,1)S(1)} %get-tuple-element.19), channel_id=1, source_target_pairs={{0,20},{2,22},{4,16},{6,18},{8,28},{10,30},{12,24},{14,26},{16,4},... | collective-permute-start | bytes 884744 | tf_op jit(solution)/shard_map/ppermute | solution.py:29
  105.7 59.1 %collective-permute-start.10 = (bf16[2,1,2,16,2304]{4,3,2,1,0:T(8,128)(2,1)S(1)}, bf16[2,1,2,16,2304]{4,3,2,1,0:T(8,128)(2,1)S(1)}, u32[]{:S(2)}, u32[]{:S(2)}) collective-permute-start(bf16[2,1,2,16,2304]{4,3,2,1,0:T(8,128)(2,1)S(1)} %get-tuple-element.18), channel_id=1, source_target_pairs={{0,22},{2,20},{4,18},{6,16},{8,30},{10,28},{12,26},{14,24},{16,6},... | collective-permute-start | bytes 884744 | tf_op jit(solution)/shard_map/ppermute | solution.py:29
  111.5 54.0 %collective-permute-start.11 = (bf16[2,1,2,16,2304]{4,3,2,1,0:T(8,128)(2,1)S(1)}, bf16[2,1,2,16,2304]{4,3,2,1,0:T(8,128)(2,1)S(1)}, u32[]{:S(2)}, u32[]{:S(2)}) collective-permute-start(bf16[2,1,2,16,2304]{4,3,2,1,0:T(8,128)(2,1)S(1)} %get-tuple-element.17), channel_id=1, source_target_pairs={{0,24},{2,26},{4,28},{6,30},{8,16},{10,18},{12,20},{14,22},{16,8},... | collective-permute-start | bytes 884744 | tf_op jit(solution)/shard_map/ppermute | solution.py:29
  114.7 51.5 %collective-permute-start.12 = (bf16[2,1,2,16,2304]{4,3,2,1,0:T(8,128)(2,1)S(1)}, bf16[2,1,2,16,2304]{4,3,2,1,0:T(8,128)(2,1)S(1)}, u32[]{:S(2)}, u32[]{:S(2)}) collective-permute-start(bf16[2,1,2,16,2304]{4,3,2,1,0:T(8,128)(2,1)S(1)} %get-tuple-element.16), channel_id=1, source_target_pairs={{0,26},{2,24},{4,30},{6,28},{8,18},{10,16},{12,22},{14,20},{16,10}... | collective-permute-start | bytes 884744 | tf_op jit(solution)/shard_map/ppermute | solution.py:29
  116.3 50.7 %collective-permute-start.13 = (bf16[2,1,2,16,2304]{4,3,2,1,0:T(8,128)(2,1)S(1)}, bf16[2,1,2,16,2304]{4,3,2,1,0:T(8,128)(2,1)S(1)}, u32[]{:S(2)}, u32[]{:S(2)}) collective-permute-start(bf16[2,1,2,16,2304]{4,3,2,1,0:T(8,128)(2,1)S(1)} %get-tuple-element.15), channel_id=1, source_target_pairs={{0,28},{2,30},{4,24},{6,26},{8,20},{10,22},{12,16},{14,18},{16,12}... | collective-permute-start | bytes 884744 | tf_op jit(solution)/shard_map/ppermute | solution.py:29
  152.0 15.7 %collective-permute-start.14 = (bf16[2,1,2,16,2304]{4,3,2,1,0:T(8,128)(2,1)S(1)}, bf16[2,1,2,16,2304]{4,3,2,1,0:T(8,128)(2,1)S(1)}, u32[]{:S(2)}, u32[]{:S(2)}) collective-permute-start(bf16[2,1,2,16,2304]{4,3,2,1,0:T(8,128)(2,1)S(1)} %get-tuple-element.14), channel_id=1, source_target_pairs={{0,30},{2,28},{4,26},{6,24},{8,22},{10,20},{12,18},{14,16},{16,14}... | collective-permute-start | bytes 884744 | tf_op jit(solution)/shard_map/ppermute | solution.py:29
  184.3 71.6 %copy-start = (bf16[128,2304]{1,0:T(8,128)(2,1)S(1)}, bf16[128,2304]{1,0:T(8,128)(2,1)}, u32[]{:S(2)}) copy-start(bf16[128,2304]{1,0:T(8,128)(2,1)} %param.10) | copy-start | bytes 1769476
  270.7 5.8 %copy-start.4 = (s32[128]{0:T(128)S(1)}, s32[128]{0:T(128)}, u32[]{:S(2)}) copy-start(s32[128]{0:T(128)} %param.9) | copy-start | bytes 1540
  270.7 92.5 %all-to-all-start.1 = ((bf16[2,16,2,16,2304]{4,3,2,0,1:T(8,128)(2,1)}), bf16[2,16,2,16,2304]{4,3,2,0,1:T(8,128)(2,1)}, u32[]{:S(2)}, u32[]{:S(2)}) async-start(bf16[2,16,2,16,2304]{4,3,2,0,1:T(8,128)(2,1)} %copy.87), calls=%async_computation.1 | async-start | bytes 9437184 | tf_op jit(solution)/shard_map/all_to_all | solution.py:101
  363.1 28.4 %all-to-all-start.3 = ((s32[2,16,2,16]{3,2,0,1:T(2,128)}), s32[2,16,2,16]{3,2,0,1:T(2,128)S(1)}, u32[]{:S(2)}, u32[]{:S(2)}) async-start(s32[2,16,2,16]{3,2,0,1:T(2,128)} %copy.92), calls=%async_computation.3 | async-start | bytes 65536 | tf_op jit(solution)/shard_map/all_to_all | solution.py:86
  384.9 12.3 %copy-start.3 = (s32[2,128,2]{1,2,0:T(2,128)S(1)}, s32[2,128,2]{1,2,0:T(2,128)}, u32[]{:S(2)}) copy-start(s32[2,128,2]{1,2,0:T(2,128)} %param.7) | copy-start | bytes 6148
  390.1 24.5 %copy-start.2 = (bf16[2,128,2,256]{3,2,1,0:T(2,128)(2,1)S(1)}, bf16[2,128,2,256]{3,2,1,0:T(2,128)(2,1)}, u32[]{:S(2)}) copy-start(bf16[2,128,2,256]{3,2,1,0:T(2,128)(2,1)} %param.6) | copy-start | bytes 786436
  391.5 19.8 %all-to-all-start.2 = ((bf16[2,16,2,16,256]{4,3,2,0,1:T(8,128)(2,1)}), bf16[2,16,2,16,256]{4,3,2,0,1:T(8,128)(2,1)S(1)}, u32[]{:S(2)}, u32[]{:S(2)}) async-start(bf16[2,16,2,16,256]{4,3,2,0,1:T(8,128)(2,1)} %copy.89), calls=%async_computation.2 | async-start | bytes 1048576 | tf_op jit(solution)/shard_map/all_to_all | solution.py:105
Sparse Core Ops, SparseCore 0:
  192.4 63.4 all-reduce.3
